TPU v7x, 32 devices: a whole 2x2x4 slice. The times are simulated.
32 devices in a mesh: row: 1, col: 16 (over z, y, core), seg: 2 (over x).
Axes of the slice: x: 2, y: 2, z: 4, core: 2. Of those that a mesh axis runs over, the one named last changes fastest.
Arguments:
- traces: bfloat16 [8, 128, 1024], P('seg', ('row', 'col')), may hold values from -600 to 600, as said below
- valid: int32 [8, 128], P('seg', ('row', 'col')), may hold values 0 or 1
Outputs:
- correlation: float32 [33, 1, 128, 128], P(None, None, ('col', 'seg'), 'row')
Inputs may be any that keep to these rules, and one draw needn't show every extreme that they name: `traces`: samples of a common wavefield delayed by up to 32 samples per station plus noise, scaled per station.
All inputs are finite; a program needn't handle non-finite values. No bound on the sum of `valid` on one device may be relied on, other than what follows from the above.
Results may differ from a plain program's by a relative error of at most 0.002.
Values may be sent and summed in bfloat16 or wider, within the bound.
No kernel may reach another device: no remote copies, remote signals or barrier semaphores. Data moves between devices by JAX's collectives and lax.ppermute only.
A program may use at most 64 MiB of HBM per device.

v0:
```python
import math
import jax
import jax.numpy as jnp
from jax import lax
from jax.sharding import PartitionSpec as P

MAXLAG = 16
LAGSET = 3


def make_tables(length, max_shift):
    bins = jnp.arange(length // 2, dtype=jnp.int32)
    samples = jnp.arange(length, dtype=jnp.int32)
    product = samples[:, None] * bins[None, :] % length
    angle = 2.0 * math.pi / length * product.astype(jnp.float32)
    dft_table = jnp.concatenate([jnp.cos(angle), -jnp.sin(angle)], axis=1).astype(jnp.bfloat16)
    shifts = jnp.arange(2 * max_shift + 1, dtype=jnp.int32) - max_shift
    lag_prod = shifts[:, None] * bins[None, :] % length
    lag_angle = 2.0 * math.pi / length * lag_prod.astype(jnp.float32)
    return (dft_table, jnp.cos(lag_angle), jnp.sin(lag_angle))


def whiten(traces, valid, dft_table):
    length = traces.shape[2]
    half = length // 2
    flat = traces.reshape(-1, length)
    spectrum = jnp.dot(flat, dft_table, preferred_element_type=jnp.float32)
    spectrum = spectrum.reshape(traces.shape[0], traces.shape[1], length)
    real_part = spectrum[..., :half]
    imag_part = spectrum[..., half:]
    power = real_part * real_part + imag_part * imag_part
    level = jnp.mean(power, axis=-1, keepdims=True)
    factor = lax.rsqrt(power + 0.1 * level + 1e-05) * valid[..., None].astype(jnp.float32)
    return jnp.concatenate([real_part * factor, imag_part * factor], axis=-1).astype(jnp.bfloat16)


def lag_sums(first_set, second_set, cosines, sines, group_size):
    half = first_set.shape[2] // 2
    lag_count = cosines.shape[0]
    real_part = second_set[..., :half].astype(jnp.float32)
    imag_part = second_set[..., half:].astype(jnp.float32)

    def one_group(group):
        cosine = lax.dynamic_slice_in_dim(cosines, group * group_size, group_size, 0)[
            :, None, None, :
        ]
        sine = lax.dynamic_slice_in_dim(sines, group * group_size, group_size, 0)[:, None, None, :]
        first = real_part[None] * cosine + imag_part[None] * sine
        second = imag_part[None] * cosine - real_part[None] * sine
        rotated = jnp.concatenate([first, second], axis=-1).astype(jnp.bfloat16)
        return jnp.einsum("gsbk,sak->gba", rotated, first_set, preferred_element_type=jnp.float32)

    result = lax.map(one_group, jnp.arange(lag_count // group_size, dtype=jnp.int32))
    return result.reshape(lag_count, second_set.shape[1], first_set.shape[1])


def on_device(traces, valid):
    length = traces.shape[2]
    dft_table, cosines, sines = make_tables(length, MAXLAG)
    whitened = whiten(traces, valid, dft_table)
    first_set = lax.all_gather(whitened, "col", axis=1, tiled=True)
    second_set = lax.all_gather(whitened, "row", axis=1, tiled=True)
    groups_row = lax.axis_size("row")
    seg_count = lax.axis_size("seg")
    segments_all = whitened.shape[0] * seg_count
    scale = 1.0 / math.sqrt(segments_all * (length // 2))
    own_count = whitened.shape[1]
    partial_value = lag_sums(first_set, second_set, cosines, sines, LAGSET)
    partial_value = partial_value.reshape(
        partial_value.shape[0], groups_row, own_count, partial_value.shape[2]
    )
    summed = lax.psum_scatter(partial_value, "seg", scatter_dimension=2, tiled=True)
    return summed * scale


def solution(mesh):
    placed = (P("seg", ("row", "col"), None), P("seg", ("row", "col")))
    return jax.shard_map(
        on_device,
        mesh=mesh,
        in_specs=placed,
        out_specs=P(None, None, ("col", "seg"), "row"),
        check_vma=False,
    )
```

profile of v0, /device:TPU:0, one launch (start us, length us, event | category | flops | bytes accessed | tf_op | source)
XLA Modules:
  0.0 119.5 jit_solution(4100799459907360552)
XLA Ops:
  6.5 8.5 %negate_convert_fusion = (bf16[1024,512]{1,0:T(8,128)(2,1)S(1)}, bf16[1024,512]{1,0:T(8,128)(2,1)S(1)}) fusion(), kind=kLoop, calls=%fused_computation.21 | loop fusion | flops 8912896 | bytes 2097152 | tf_op jit(solution)/shard_map/convert.5
  15.9 0.6 pad_maximum_fusion
  17.0 40.3 %all-gather.2.cloned.1.call-done = bf16[4,128,1024]{2,1,0:T(8,128)(2,1)} async-done(((bf16[4,8,1024]{2,1,0:T(8,128)(2,1)}), bf16[4,128,1024]{2,1,0:T(8,128)(2,1)}) %all-gather.2.cloned.1.call-update) | async-done | bytes 1048592 | tf_op jit(solution)/shard_map/all_gather | solution.py:61
  57.3 32.3 %while.10 = (s32[]{:T(128)}, f32[11,3,8,128]{3,2,1,0:T(8,128)S(1)}, f32[4,8,512]{2,1,0:T(8,128)S(1)}, s32[11]{0:T(128)S(1)}, f32[33,512]{1,0:T(8,128)S(1)}, /*in...) while((s32[]{:T(128)}, f32[11,3,8,128]{3,2,1,0:T(8,128)S(1)}, ...), condition=%wide.region_2.3_spmd, body=%wide.region_1.2_spmd.sunk | while | flops 25952260 | bytes 1622199 | solution.py:53
  58.6 1.6 %fusion.37 = f32[11,3,8,128]{3,2,1,0:T(8,128)S(1)} fusion(f32[11,3,8,128]{3,2,1,0:T(8,128)S(1)} %get-tuple-element.148, s32[]{:T(128)} %get-tuple-element.147, bf16[4,128,1024]{2,1,0:T(8,128)(2,1)} %get-tuple-element.166, bf16[3,4,8,512]{3,2,1,0:T(8,128)(2,1)S(1)} %get-tuple-element.133, bf16[3,4,8,512]{3,2,1,0:T(8,128)(2,1)S(1)} %get-tuple-element.134), kind=kOutput, calls=%fused_computation.1.clone.1 | convolution fusion | flops 25559040 | bytes 1257476 | tf_op jit(solution)/shard_map/while/body/eval_jaxpr/gsbk,sak->gba/dot_general | solution.py:51
  60.2 0.6 dynamic_slice.15
  61.5 1.6 %fusion.37 = f32[11,3,8,128]{3,2,1,0:T(8,128)S(1)} fusion(f32[11,3,8,128]{3,2,1,0:T(8,128)S(1)} %get-tuple-element.148, s32[]{:T(128)} %get-tuple-element.147, bf16[4,128,1024]{2,1,0:T(8,128)(2,1)} %get-tuple-element.166, bf16[3,4,8,512]{3,2,1,0:T(8,128)(2,1)S(1)} %get-tuple-element.133, bf16[3,4,8,512]{3,2,1,0:T(8,128)(2,1)S(1)} %get-tuple-element.134), kind=kOutput, calls=%fused_computation.1.clone.1 | convolution fusion | flops 25559040 | bytes 1257476 | tf_op jit(solution)/shard_map/while/body/eval_jaxpr/gsbk,sak->gba/dot_general | solution.py:51
  63.2 0.6 dynamic_slice.15
  64.5 1.6 %fusion.37 = f32[11,3,8,128]{3,2,1,0:T(8,128)S(1)} fusion(f32[11,3,8,128]{3,2,1,0:T(8,128)S(1)} %get-tuple-element.148, s32[]{:T(128)} %get-tuple-element.147, bf16[4,128,1024]{2,1,0:T(8,128)(2,1)} %get-tuple-element.166, bf16[3,4,8,512]{3,2,1,0:T(8,128)(2,1)S(1)} %get-tuple-element.133, bf16[3,4,8,512]{3,2,1,0:T(8,128)(2,1)S(1)} %get-tuple-element.134), kind=kOutput, calls=%fused_computation.1.clone.1 | convolution fusion | flops 25559040 | bytes 1257476 | tf_op jit(solution)/shard_map/while/body/eval_jaxpr/gsbk,sak->gba/dot_general | solution.py:51
  66.1 0.6 dynamic_slice.15
  67.4 1.6 %fusion.37 = f32[11,3,8,128]{3,2,1,0:T(8,128)S(1)} fusion(f32[11,3,8,128]{3,2,1,0:T(8,128)S(1)} %get-tuple-element.148, s32[]{:T(128)} %get-tuple-element.147, bf16[4,128,1024]{2,1,0:T(8,128)(2,1)} %get-tuple-element.166, bf16[3,4,8,512]{3,2,1,0:T(8,128)(2,1)S(1)} %get-tuple-element.133, bf16[3,4,8,512]{3,2,1,0:T(8,128)(2,1)S(1)} %get-tuple-element.134), kind=kOutput, calls=%fused_computation.1.clone.1 | convolution fusion | flops 25559040 | bytes 1257476 | tf_op jit(solution)/shard_map/while/body/eval_jaxpr/gsbk,sak->gba/dot_general | solution.py:51
  69.0 0.6 dynamic_slice.15
  70.4 1.6 %fusion.37 = f32[11,3,8,128]{3,2,1,0:T(8,128)S(1)} fusion(f32[11,3,8,128]{3,2,1,0:T(8,128)S(1)} %get-tuple-element.148, s32[]{:T(128)} %get-tuple-element.147, bf16[4,128,1024]{2,1,0:T(8,128)(2,1)} %get-tuple-element.166, bf16[3,4,8,512]{3,2,1,0:T(8,128)(2,1)S(1)} %get-tuple-element.133, bf16[3,4,8,512]{3,2,1,0:T(8,128)(2,1)S(1)} %get-tuple-element.134), kind=kOutput, calls=%fused_computation.1.clone.1 | convolution fusion | flops 25559040 | bytes 1257476 | tf_op jit(solution)/shard_map/while/body/eval_jaxpr/gsbk,sak->gba/dot_general | solution.py:51
  72.0 0.6 dynamic_slice.15
  73.3 1.6 %fusion.37 = f32[11,3,8,128]{3,2,1,0:T(8,128)S(1)} fusion(f32[11,3,8,128]{3,2,1,0:T(8,128)S(1)} %get-tuple-element.148, s32[]{:T(128)} %get-tuple-element.147, bf16[4,128,1024]{2,1,0:T(8,128)(2,1)} %get-tuple-element.166, bf16[3,4,8,512]{3,2,1,0:T(8,128)(2,1)S(1)} %get-tuple-element.133, bf16[3,4,8,512]{3,2,1,0:T(8,128)(2,1)S(1)} %get-tuple-element.134), kind=kOutput, calls=%fused_computation.1.clone.1 | convolution fusion | flops 25559040 | bytes 1257476 | tf_op jit(solution)/shard_map/while/body/eval_jaxpr/gsbk,sak->gba/dot_general | solution.py:51
  74.9 0.6 dynamic_slice.15
  76.3 1.6 %fusion.37 = f32[11,3,8,128]{3,2,1,0:T(8,128)S(1)} fusion(f32[11,3,8,128]{3,2,1,0:T(8,128)S(1)} %get-tuple-element.148, s32[]{:T(128)} %get-tuple-element.147, bf16[4,128,1024]{2,1,0:T(8,128)(2,1)} %get-tuple-element.166, bf16[3,4,8,512]{3,2,1,0:T(8,128)(2,1)S(1)} %get-tuple-element.133, bf16[3,4,8,512]{3,2,1,0:T(8,128)(2,1)S(1)} %get-tuple-element.134), kind=kOutput, calls=%fused_computation.1.clone.1 | convolution fusion | flops 25559040 | bytes 1257476 | tf_op jit(solution)/shard_map/while/body/eval_jaxpr/gsbk,sak->gba/dot_general | solution.py:51
  79.2 1.6 %fusion.37 = f32[11,3,8,128]{3,2,1,0:T(8,128)S(1)} fusion(f32[11,3,8,128]{3,2,1,0:T(8,128)S(1)} %get-tuple-element.148, s32[]{:T(128)} %get-tuple-element.147, bf16[4,128,1024]{2,1,0:T(8,128)(2,1)} %get-tuple-element.166, bf16[3,4,8,512]{3,2,1,0:T(8,128)(2,1)S(1)} %get-tuple-element.133, bf16[3,4,8,512]{3,2,1,0:T(8,128)(2,1)S(1)} %get-tuple-element.134), kind=kOutput, calls=%fused_computation.1.clone.1 | convolution fusion | flops 25559040 | bytes 1257476 | tf_op jit(solution)/shard_map/while/body/eval_jaxpr/gsbk,sak->gba/dot_general | solution.py:51
  82.1 1.6 %fusion.37 = f32[11,3,8,128]{3,2,1,0:T(8,128)S(1)} fusion(f32[11,3,8,128]{3,2,1,0:T(8,128)S(1)} %get-tuple-element.148, s32[]{:T(128)} %get-tuple-element.147, bf16[4,128,1024]{2,1,0:T(8,128)(2,1)} %get-tuple-element.166, bf16[3,4,8,512]{3,2,1,0:T(8,128)(2,1)S(1)} %get-tuple-element.133, bf16[3,4,8,512]{3,2,1,0:T(8,128)(2,1)S(1)} %get-tuple-element.134), kind=kOutput, calls=%fused_computation.1.clone.1 | convolution fusion | flops 25559040 | bytes 1257476 | tf_op jit(solution)/shard_map/while/body/eval_jaxpr/gsbk,sak->gba/dot_general | solution.py:51
  85.1 1.6 %fusion.37 = f32[11,3,8,128]{3,2,1,0:T(8,128)S(1)} fusion(f32[11,3,8,128]{3,2,1,0:T(8,128)S(1)} %get-tuple-element.148, s32[]{:T(128)} %get-tuple-element.147, bf16[4,128,1024]{2,1,0:T(8,128)(2,1)} %get-tuple-element.166, bf16[3,4,8,512]{3,2,1,0:T(8,128)(2,1)S(1)} %get-tuple-element.133, bf16[3,4,8,512]{3,2,1,0:T(8,128)(2,1)S(1)} %get-tuple-element.134), kind=kOutput, calls=%fused_computation.1.clone.1 | convolution fusion | flops 25559040 | bytes 1257476 | tf_op jit(solution)/shard_map/while/body/eval_jaxpr/gsbk,sak->gba/dot_general | solution.py:51
  88.0 1.6 %fusion.37 = f32[11,3,8,128]{3,2,1,0:T(8,128)S(1)} fusion(f32[11,3,8,128]{3,2,1,0:T(8,128)S(1)} %get-tuple-element.148, s32[]{:T(128)} %get-tuple-element.147, bf16[4,128,1024]{2,1,0:T(8,128)(2,1)} %get-tuple-element.166, bf16[3,4,8,512]{3,2,1,0:T(8,128)(2,1)S(1)} %get-tuple-element.133, bf16[3,4,8,512]{3,2,1,0:T(8,128)(2,1)S(1)} %get-tuple-element.134), kind=kOutput, calls=%fused_computation.1.clone.1 | convolution fusion | flops 25559040 | bytes 1257476 | tf_op jit(solution)/shard_map/while/body/eval_jaxpr/gsbk,sak->gba/dot_general | solution.py:51
  89.6 0.6 copy-done.1
  91.6 19.5 %all-reduce.3.cloned.1.call-done = f32[33,1,8,128]{3,2,1,0:T(8,128)} async-done(((f32[33,1,8,128]{3,2,1,0:T(8,128)}), f32[33,1,8,128]{3,2,1,0:T(8,128)}) %all-reduce.3.cloned.1.call-update) | async-done | bytes 135184
  111.1 1.6 %dynamic-slice_multiply_fusion = f32[33,1,4,128]{3,2,1,0:T(4,128)} fusion(f32[33,1,8,128]{3,2,1,0:T(8,128)} %all-reduce.3.cloned.1.call-done, u32[]{:T(128)S(6)} %multiply.4), kind=kLoop, calls=%fused_computation.36 | loop fusion | flops 16896 | bytes 135172 | tf_op jit(solution)/shard_map/mul | solution.py:73
  (48 shorter events, 5.5 us)
Async XLA Ops:
  6.5 8.6 %copy-start = (bf16[4,8,1024]{2,1,0:T(8,128)(2,1)S(1)}, bf16[4,8,1024]{2,1,0:T(8,128)(2,1)}, u32[]{:S(2)}) copy-start(bf16[4,8,1024]{2,1,0:T(8,128)(2,1)} %param.4) | copy-start | bytes 196612
  6.5 50.7 %all-gather.2.cloned.1.call-start = ((), (), s32[]{:S(2)}) async-start(), calls=%async_computation | async-start | bytes 1114112 | tf_op jit(solution)/shard_map/all_gather | solution.py:61
  15.1 0.7 copy-start.2
  16.5 94.5 %all-reduce.3.cloned.1.call-start = ((), (), s32[]{:S(2)}) async-start(), calls=%async_computation.1 | async-start | bytes 270336
  57.3 33.0 %copy-start.3 = (u32[32]{0:T(128)S(1)}, u32[32]{0:T(128)}, u32[]{:S(2)}) copy-start(u32[32]{0:T(128)} %constant.59) | copy-start | bytes 388
  89.6 0.7 copy-start.1
Sparse Core Ops, SparseCore 0:
  16.7 40.5 all-gather.1
  90.4 20.5 all-reduce.2
where the time goes:
time: 120 us; the launch traced here: 119 us
  waiting for transfers between devices  59.8 us (50%)
  matrix products  18.1 us (15%)
  between operations  14.1 us (12%)
  other arithmetic  11.9 us (10%)
  local copies, waits for them, and re-layouts  8.06 us (7%)
  loops' own time  7.39 us (6%)
    all_gather x1, waiting for transfers between devices, on_device(): first_set = lax.all_gather(whitened, 'col', axis=1, tiled=True)  40.3 us
    unnamed x3, waiting for transfers between devices  19.5 us
    dot_general x11, matrix products, one_group(): jnp.einsum('gsbk,sak->gba', rotated, first_set, preferred_element_type=jn...  17.7 us
    another operation x12, other arithmetic  9.11 us
    another operation x1, loops' own time, lag_sums(): lax.map(one_group, jnp.arange(lag_count // group_size, dtype=jnp.int32))  7.39 us
    dynamic_slice x11, local copies, waits for them, and re-layouts, lag_sums(): lax.map(one_group, jnp.arange(lag_count // group_size, dtype=jnp.int32))  6.54 us
  transfers between devices with their start and end apart: 2, of which 2 were waited for; matrix products, arithmetic and copies ran while one was open for 1% of the time, Pallas kernels for 0%

commit v1 on v0

--- a/solution.py
+++ b/solution.py
@@ -58,7 +58,24 @@
     length = traces.shape[2]
     dft_table, cosines, sines = make_tables(length, MAXLAG)
     whitened = whiten(traces, valid, dft_table)
-    first_set = lax.all_gather(whitened, "col", axis=1, tiled=True)
+    val2, v1, res = (lax.axis_size("col"), lax.axis_index("col"), whitened.shape[1])
+    crops = [i * val2 if m == 1 else i for m, i in enumerate(whitened.shape)]
+    first_set = lax.dynamic_update_slice_in_dim(
+        jnp.zeros(crops, whitened.dtype), whitened, v1 * res, axis=1
+    )
+    p_next = seen_now = whitened
+    for k in range(1, val2 // 2 + 1):
+        p_next = lax.ppermute(
+            p_next, axis_name="col", perm=[(m, (m + 1) % val2) for m in range(val2)]
+        )
+        first_set = lax.dynamic_update_slice_in_dim(
+            first_set, p_next, (v1 - k) % val2 * res, axis=1
+        )
+        if 2 * k < val2:
+            seen_now = lax.ppermute(seen_now, "col", [(m, (m - 1) % val2) for m in range(val2)])
+            first_set = lax.dynamic_update_slice_in_dim(
+                first_set, seen_now, (v1 + k) % val2 * res, axis=1
+            )
     second_set = lax.all_gather(whitened, "row", axis=1, tiled=True)
     groups_row = lax.axis_size("row")
     seg_count = lax.axis_size("seg")

time: 120 us -> 116 us (0.967)
  starting transfers between devices: 0.04 us -> 32.4 us
  waiting for transfers between devices: 59.8 us -> 37 us
  matrix products: 18.1 us -> 4.69 us
    all_gather x1 -> x0, waiting for transfers between devices: 40.3 us -> none  [on_device(): first_set = lax.all_gather(whitened, 'col', axis=1, tiled=True)]
    ppermute x0 -> x15, starting transfers between devices: none -> 32.4 us  [the longest x7 31.9 us: on_device(): lax.ppermute(seen_now, 'col', [(m, (m - 1) % val2) for m in range(val2)])]
    ppermute x0 -> x15, waiting for transfers between devices: none -> 18.9 us  [the longest x8 18.8 us: on_device(): lax.ppermute(p_next, axis_name='col', perm=[(m, (m + 1) % val2) for m in...]
    dot_general x11, matrix products: 17.7 us -> 4.24 us  [one_group(): jnp.einsum('gsbk,sak->gba', rotated, first_set, preferred_element_type=jn...]
    unnamed x3 -> x2, waiting for transfers between devices: 19.5 us -> 18.1 us
  transfers between devices with their start and end apart: 2 -> 16, of which waited for: 2 -> 9; matrix products, arithmetic and copies ran while one was open for 1% -> 1% of each run, Pallas kernels for 0% -> 0%
where the time goes in v1:
time: 116 us
  waiting for transfers between devices  37 us (32%)
  starting transfers between devices  32.4 us (28%)
  between operations  14.6 us (13%)
  other arithmetic  11.3 us (10%)
  local copies, waits for them, and re-layouts  9 us (8%)
  loops' own time  7.14 us (6%)
  matrix products  4.69 us (4%)
    ppermute x7, starting transfers between devices, on_device(): lax.ppermute(seen_now, 'col', [(m, (m - 1) % val2) for m in range(val2)])  31.9 us
    ppermute x8, waiting for transfers between devices, on_device(): lax.ppermute(p_next, axis_name='col', perm=[(m, (m + 1) % val2) for m in...  18.8 us
    unnamed x2, waiting for transfers between devices  18.1 us
    another operation x12, other arithmetic  9.11 us
    dynamic_slice x11, local copies, waits for them, and re-layouts, lag_sums(): lax.map(one_group, jnp.arange(lag_count // group_size, dtype=jnp.int32))  7.21 us
    another operation x1, loops' own time, lag_sums(): lax.map(one_group, jnp.arange(lag_count // group_size, dtype=jnp.int32))  7.14 us
    dot_general x11, matrix products, one_group(): jnp.einsum('gsbk,sak->gba', rotated, first_set, preferred_element_type=jn...  4.24 us
  transfers between devices with their start and end apart: 16, of which 9 were waited for; matrix products, arithmetic and copies ran while one was open for 1% of the time, Pallas kernels for 0%

profile of v1, /device:TPU:0, one launch (start us, length us, event | category | flops | bytes accessed | tf_op | source)
XLA Modules:
  0.0 116.1 jit_solution(4058628714386787145)
XLA Ops:
  6.5 8.5 %negate_convert_fusion = (bf16[1024,512]{1,0:T(8,128)(2,1)S(1)}, bf16[1024,512]{1,0:T(8,128)(2,1)S(1)}) fusion(), kind=kLoop, calls=%fused_computation.21 | loop fusion | flops 8912896 | bytes 2097152 | tf_op jit(solution)/shard_map/convert.5
  16.6 5.0 %collective-permute-start.1 = (bf16[4,8,1024]{2,1,0:T(8,128)(2,1)S(1)}, bf16[4,8,1024]{2,1,0:T(8,128)(2,1)S(1)}, u32[]{:S(2)}, u32[]{:S(2)}) collective-permute-start(bf16[4,8,1024]{2,1,0:T(8,128)(2,1)S(1)} %get-tuple-element.74), channel_id=1, source_target_pairs={{0,30},{2,0},{4,2},{6,4},{8,6},{10,8},{12,10},{14,12},{16,14},{18,... | collective-permute-start | bytes 196616 | tf_op jit(solution)/shard_map/ppermute | solution.py:75
  22.4 1.2 %collective-permute-done = bf16[4,8,1024]{2,1,0:T(8,128)(2,1)S(1)} collective-permute-done((bf16[4,8,1024]{2,1,0:T(8,128)(2,1)S(1)}, bf16[4,8,1024]{2,1,0:T(8,128)(2,1)S(1)}, u32[]{:S(2)}, u32[]{:S(2)}) %collective-permute-start) | collective-permute-done | bytes 65568 | tf_op jit(solution)/shard_map/ppermute | solution.py:68
  23.6 4.4 %collective-permute-start.3 = (bf16[4,8,1024]{2,1,0:T(8,128)(2,1)S(1)}, bf16[4,8,1024]{2,1,0:T(8,128)(2,1)S(1)}, u32[]{:S(2)}, u32[]{:S(2)}) collective-permute-start(bf16[4,8,1024]{2,1,0:T(8,128)(2,1)S(1)} %collective-permute-done.1), channel_id=1, source_target_pairs={{0,30},{2,0},{4,2},{6,4},{8,6},{10,8},{12,10},{14,12},{16,14},{18,... | collective-permute-start | bytes 196616 | tf_op jit(solution)/shard_map/ppermute | solution.py:75
  28.1 1.9 %collective-permute-done.2 = bf16[4,8,1024]{2,1,0:T(8,128)(2,1)S(1)} collective-permute-done((bf16[4,8,1024]{2,1,0:T(8,128)(2,1)S(1)}, bf16[4,8,1024]{2,1,0:T(8,128)(2,1)S(1)}, u32[]{:S(2)}, u32[]{:S(2)}) %collective-permute-start.2) | collective-permute-done | bytes 65568 | tf_op jit(solution)/shard_map/ppermute | solution.py:68
  30.0 4.4 %collective-permute-start.5 = (bf16[4,8,1024]{2,1,0:T(8,128)(2,1)S(1)}, bf16[4,8,1024]{2,1,0:T(8,128)(2,1)S(1)}, u32[]{:S(2)}, u32[]{:S(2)}) collective-permute-start(bf16[4,8,1024]{2,1,0:T(8,128)(2,1)S(1)} %collective-permute-done.3), channel_id=1, source_target_pairs={{0,30},{2,0},{4,2},{6,4},{8,6},{10,8},{12,10},{14,12},{16,14},{18,... | collective-permute-start | bytes 196616 | tf_op jit(solution)/shard_map/ppermute | solution.py:75
  34.5 1.9 %collective-permute-done.4 = bf16[4,8,1024]{2,1,0:T(8,128)(2,1)S(1)} collective-permute-done((bf16[4,8,1024]{2,1,0:T(8,128)(2,1)S(1)}, bf16[4,8,1024]{2,1,0:T(8,128)(2,1)S(1)}, u32[]{:S(2)}, u32[]{:S(2)}) %collective-permute-start.4) | collective-permute-done | bytes 65568 | tf_op jit(solution)/shard_map/ppermute | solution.py:68
  36.4 4.5 %collective-permute-start.7 = (bf16[4,8,1024]{2,1,0:T(8,128)(2,1)S(1)}, bf16[4,8,1024]{2,1,0:T(8,128)(2,1)S(1)}, u32[]{:S(2)}, u32[]{:S(2)}) collective-permute-start(bf16[4,8,1024]{2,1,0:T(8,128)(2,1)S(1)} %collective-permute-done.5), channel_id=1, source_target_pairs={{0,30},{2,0},{4,2},{6,4},{8,6},{10,8},{12,10},{14,12},{16,14},{18,... | collective-permute-start | bytes 196616 | tf_op jit(solution)/shard_map/ppermute | solution.py:75
  40.9 1.9 %collective-permute-done.6 = bf16[4,8,1024]{2,1,0:T(8,128)(2,1)S(1)} collective-permute-done((bf16[4,8,1024]{2,1,0:T(8,128)(2,1)S(1)}, bf16[4,8,1024]{2,1,0:T(8,128)(2,1)S(1)}, u32[]{:S(2)}, u32[]{:S(2)}) %collective-permute-start.6) | collective-permute-done | bytes 65568 | tf_op jit(solution)/shard_map/ppermute | solution.py:68
  42.8 4.5 %collective-permute-start.9 = (bf16[4,8,1024]{2,1,0:T(8,128)(2,1)S(1)}, bf16[4,8,1024]{2,1,0:T(8,128)(2,1)S(1)}, u32[]{:S(2)}, u32[]{:S(2)}) collective-permute-start(bf16[4,8,1024]{2,1,0:T(8,128)(2,1)S(1)} %collective-permute-done.7), channel_id=1, source_target_pairs={{0,30},{2,0},{4,2},{6,4},{8,6},{10,8},{12,10},{14,12},{16,14},{18,... | collective-permute-start | bytes 196616 | tf_op jit(solution)/shard_map/ppermute | solution.py:75
  47.3 1.9 %collective-permute-done.8 = bf16[4,8,1024]{2,1,0:T(8,128)(2,1)S(1)} collective-permute-done((bf16[4,8,1024]{2,1,0:T(8,128)(2,1)S(1)}, bf16[4,8,1024]{2,1,0:T(8,128)(2,1)S(1)}, u32[]{:S(2)}, u32[]{:S(2)}) %collective-permute-start.8) | collective-permute-done | bytes 65568 | tf_op jit(solution)/shard_map/ppermute | solution.py:68
  49.2 4.5 %collective-permute-start.11 = (bf16[4,8,1024]{2,1,0:T(8,128)(2,1)S(1)}, bf16[4,8,1024]{2,1,0:T(8,128)(2,1)S(1)}, u32[]{:S(2)}, u32[]{:S(2)}) collective-permute-start(bf16[4,8,1024]{2,1,0:T(8,128)(2,1)S(1)} %collective-permute-done.9), channel_id=1, source_target_pairs={{0,30},{2,0},{4,2},{6,4},{8,6},{10,8},{12,10},{14,12},{16,14},{18,... | collective-permute-start | bytes 196616 | tf_op jit(solution)/shard_map/ppermute | solution.py:75
  53.7 1.9 %collective-permute-done.10 = bf16[4,8,1024]{2,1,0:T(8,128)(2,1)S(1)} collective-permute-done((bf16[4,8,1024]{2,1,0:T(8,128)(2,1)S(1)}, bf16[4,8,1024]{2,1,0:T(8,128)(2,1)S(1)}, u32[]{:S(2)}, u32[]{:S(2)}) %collective-permute-start.10) | collective-permute-done | bytes 65568 | tf_op jit(solution)/shard_map/ppermute | solution.py:68
  55.6 4.5 %collective-permute-start.13 = (bf16[4,8,1024]{2,1,0:T(8,128)(2,1)S(1)}, bf16[4,8,1024]{2,1,0:T(8,128)(2,1)S(1)}, u32[]{:S(2)}, u32[]{:S(2)}) collective-permute-start(bf16[4,8,1024]{2,1,0:T(8,128)(2,1)S(1)} %collective-permute-done.11), channel_id=1, source_target_pairs={{0,30},{2,0},{4,2},{6,4},{8,6},{10,8},{12,10},{14,12},{16,14},{18,... | collective-permute-start | bytes 196616 | tf_op jit(solution)/shard_map/ppermute | solution.py:75
  60.1 1.9 %collective-permute-done.12 = bf16[4,8,1024]{2,1,0:T(8,128)(2,1)S(1)} collective-permute-done((bf16[4,8,1024]{2,1,0:T(8,128)(2,1)S(1)}, bf16[4,8,1024]{2,1,0:T(8,128)(2,1)S(1)}, u32[]{:S(2)}, u32[]{:S(2)}) %collective-permute-start.12) | collective-permute-done | bytes 65568 | tf_op jit(solution)/shard_map/ppermute | solution.py:68
  62.0 6.3 %collective-permute-done.14 = bf16[4,8,1024]{2,1,0:T(8,128)(2,1)S(1)} collective-permute-done((bf16[4,8,1024]{2,1,0:T(8,128)(2,1)S(1)}, bf16[4,8,1024]{2,1,0:T(8,128)(2,1)S(1)}, u32[]{:S(2)}, u32[]{:S(2)}) %collective-permute-start.14) | collective-permute-done | bytes 65568 | tf_op jit(solution)/shard_map/ppermute | solution.py:68
  68.4 19.3 %while.10 = (s32[]{:T(128)}, f32[11,3,8,128]{3,2,1,0:T(8,128)S(1)}, f32[4,8,512]{2,1,0:T(8,128)S(1)}, s32[11]{0:T(128)S(1)}, f32[33,512]{1,0:T(8,128)S(1)}, /*in...) while((s32[]{:T(128)}, f32[11,3,8,128]{3,2,1,0:T(8,128)S(1)}, ...), condition=%wide.region_2.3_spmd, body=%wide.region_1.2_spmd.sunk | while | flops 25952260 | bytes 1622199 | solution.py:53
  70.1 0.7 dynamic_slice.15
  75.4 0.7 dynamic_slice.15
  80.7 0.7 dynamic_slice.15
  82.4 0.7 dynamic_slice.15
  84.2 0.7 dynamic_slice.15
  89.6 18.1 %all-reduce.3.cloned.1.call-done = f32[33,1,8,128]{3,2,1,0:T(8,128)} async-done(((f32[33,1,8,128]{3,2,1,0:T(8,128)}), f32[33,1,8,128]{3,2,1,0:T(8,128)}) %all-reduce.3.cloned.1.call-update) | async-done | bytes 135184
  107.7 1.6 %dynamic-slice_multiply_fusion = f32[33,1,4,128]{3,2,1,0:T(4,128)} fusion(f32[33,1,8,128]{3,2,1,0:T(8,128)} %all-reduce.3.cloned.1.call-done, u32[]{:T(128)S(6)} %multiply.4), kind=kLoop, calls=%fused_computation.36 | loop fusion | flops 16896 | bytes 135172 | tf_op jit(solution)/shard_map/mul | solution.py:90
  (91 shorter events, 12.2 us)
Async XLA Ops:
  6.5 8.6 %copy-start = (bf16[4,8,1024]{2,1,0:T(8,128)(2,1)S(1)}, bf16[4,8,1024]{2,1,0:T(8,128)(2,1)}, u32[]{:S(2)}) copy-start(bf16[4,8,1024]{2,1,0:T(8,128)(2,1)} %param.4) | copy-start | bytes 196612
  6.5 101.2 %all-reduce.3.cloned.1.call-start = ((), (), s32[]{:S(2)}) async-start(), calls=%async_computation | async-start | bytes 270336
  15.1 0.7 copy-start.2
  16.0 7.6 %collective-permute-start = (bf16[4,8,1024]{2,1,0:T(8,128)(2,1)S(1)}, bf16[4,8,1024]{2,1,0:T(8,128)(2,1)S(1)}, u32[]{:S(2)}, u32[]{:S(2)}) collective-permute-start(bf16[4,8,1024]{2,1,0:T(8,128)(2,1)S(1)} %get-tuple-element.74), channel_id=1, source_target_pairs={{0,2},{2,4},{4,6},{6,8},{8,10},{10,12},{12,14},{14,16},{16,18},{18... | collective-permute-start | bytes 196616 | tf_op jit(solution)/shard_map/ppermute | solution.py:68
  16.6 7.0 %collective-permute-start.1 = (bf16[4,8,1024]{2,1,0:T(8,128)(2,1)S(1)}, bf16[4,8,1024]{2,1,0:T(8,128)(2,1)S(1)}, u32[]{:S(2)}, u32[]{:S(2)}) collective-permute-start(bf16[4,8,1024]{2,1,0:T(8,128)(2,1)S(1)} %get-tuple-element.74), channel_id=1, source_target_pairs={{0,30},{2,0},{4,2},{6,4},{8,6},{10,8},{12,10},{14,12},{16,14},{18,... | collective-permute-start | bytes 196616 | tf_op jit(solution)/shard_map/ppermute | solution.py:75
  23.6 6.4 %collective-permute-start.2 = (bf16[4,8,1024]{2,1,0:T(8,128)(2,1)S(1)}, bf16[4,8,1024]{2,1,0:T(8,128)(2,1)S(1)}, u32[]{:S(2)}, u32[]{:S(2)}) collective-permute-start(bf16[4,8,1024]{2,1,0:T(8,128)(2,1)S(1)} %collective-permute-done), channel_id=1, source_target_pairs={{0,2},{2,4},{4,6},{6,8},{8,10},{10,12},{12,14},{14,16},{16,18},{18... | collective-permute-start | bytes 196616 | tf_op jit(solution)/shard_map/ppermute | solution.py:68
  23.6 6.4 %collective-permute-start.3 = (bf16[4,8,1024]{2,1,0:T(8,128)(2,1)S(1)}, bf16[4,8,1024]{2,1,0:T(8,128)(2,1)S(1)}, u32[]{:S(2)}, u32[]{:S(2)}) collective-permute-start(bf16[4,8,1024]{2,1,0:T(8,128)(2,1)S(1)} %collective-permute-done.1), channel_id=1, source_target_pairs={{0,30},{2,0},{4,2},{6,4},{8,6},{10,8},{12,10},{14,12},{16,14},{18,... | collective-permute-start | bytes 196616 | tf_op jit(solution)/shard_map/ppermute | solution.py:75
  30.0 6.4 %collective-permute-start.4 = (bf16[4,8,1024]{2,1,0:T(8,128)(2,1)S(1)}, bf16[4,8,1024]{2,1,0:T(8,128)(2,1)S(1)}, u32[]{:S(2)}, u32[]{:S(2)}) collective-permute-start(bf16[4,8,1024]{2,1,0:T(8,128)(2,1)S(1)} %collective-permute-done.2), channel_id=1, source_target_pairs={{0,2},{2,4},{4,6},{6,8},{8,10},{10,12},{12,14},{14,16},{16,18},{18... | collective-permute-start | bytes 196616 | tf_op jit(solution)/shard_map/ppermute | solution.py:68
  30.0 6.4 %collective-permute-start.5 = (bf16[4,8,1024]{2,1,0:T(8,128)(2,1)S(1)}, bf16[4,8,1024]{2,1,0:T(8,128)(2,1)S(1)}, u32[]{:S(2)}, u32[]{:S(2)}) collective-permute-start(bf16[4,8,1024]{2,1,0:T(8,128)(2,1)S(1)} %collective-permute-done.3), channel_id=1, source_target_pairs={{0,30},{2,0},{4,2},{6,4},{8,6},{10,8},{12,10},{14,12},{16,14},{18,... | collective-permute-start | bytes 196616 | tf_op jit(solution)/shard_map/ppermute | solution.py:75
  36.4 6.4 %collective-permute-start.6 = (bf16[4,8,1024]{2,1,0:T(8,128)(2,1)S(1)}, bf16[4,8,1024]{2,1,0:T(8,128)(2,1)S(1)}, u32[]{:S(2)}, u32[]{:S(2)}) collective-permute-start(bf16[4,8,1024]{2,1,0:T(8,128)(2,1)S(1)} %collective-permute-done.4), channel_id=1, source_target_pairs={{0,2},{2,4},{4,6},{6,8},{8,10},{10,12},{12,14},{14,16},{16,18},{18... | collective-permute-start | bytes 196616 | tf_op jit(solution)/shard_map/ppermute | solution.py:68
  36.4 6.4 %collective-permute-start.7 = (bf16[4,8,1024]{2,1,0:T(8,128)(2,1)S(1)}, bf16[4,8,1024]{2,1,0:T(8,128)(2,1)S(1)}, u32[]{:S(2)}, u32[]{:S(2)}) collective-permute-start(bf16[4,8,1024]{2,1,0:T(8,128)(2,1)S(1)} %collective-permute-done.5), channel_id=1, source_target_pairs={{0,30},{2,0},{4,2},{6,4},{8,6},{10,8},{12,10},{14,12},{16,14},{18,... | collective-permute-start | bytes 196616 | tf_op jit(solution)/shard_map/ppermute | solution.py:75
  42.8 6.4 %collective-permute-start.8 = (bf16[4,8,1024]{2,1,0:T(8,128)(2,1)S(1)}, bf16[4,8,1024]{2,1,0:T(8,128)(2,1)S(1)}, u32[]{:S(2)}, u32[]{:S(2)}) collective-permute-start(bf16[4,8,1024]{2,1,0:T(8,128)(2,1)S(1)} %collective-permute-done.6), channel_id=1, source_target_pairs={{0,2},{2,4},{4,6},{6,8},{8,10},{10,12},{12,14},{14,16},{16,18},{18... | collective-permute-start | bytes 196616 | tf_op jit(solution)/shard_map/ppermute | solution.py:68
  42.8 6.4 %collective-permute-start.9 = (bf16[4,8,1024]{2,1,0:T(8,128)(2,1)S(1)}, bf16[4,8,1024]{2,1,0:T(8,128)(2,1)S(1)}, u32[]{:S(2)}, u32[]{:S(2)}) collective-permute-start(bf16[4,8,1024]{2,1,0:T(8,128)(2,1)S(1)} %collective-permute-done.7), channel_id=1, source_target_pairs={{0,30},{2,0},{4,2},{6,4},{8,6},{10,8},{12,10},{14,12},{16,14},{18,... | collective-permute-start | bytes 196616 | tf_op jit(solution)/shard_map/ppermute | solution.py:75
  49.2 6.4 %collective-permute-start.10 = (bf16[4,8,1024]{2,1,0:T(8,128)(2,1)S(1)}, bf16[4,8,1024]{2,1,0:T(8,128)(2,1)S(1)}, u32[]{:S(2)}, u32[]{:S(2)}) collective-permute-start(bf16[4,8,1024]{2,1,0:T(8,128)(2,1)S(1)} %collective-permute-done.8), channel_id=1, source_target_pairs={{0,2},{2,4},{4,6},{6,8},{8,10},{10,12},{12,14},{14,16},{16,18},{18... | collective-permute-start | bytes 196616 | tf_op jit(solution)/shard_map/ppermute | solution.py:68
  49.2 6.4 %collective-permute-start.11 = (bf16[4,8,1024]{2,1,0:T(8,128)(2,1)S(1)}, bf16[4,8,1024]{2,1,0:T(8,128)(2,1)S(1)}, u32[]{:S(2)}, u32[]{:S(2)}) collective-permute-start(bf16[4,8,1024]{2,1,0:T(8,128)(2,1)S(1)} %collective-permute-done.9), channel_id=1, source_target_pairs={{0,30},{2,0},{4,2},{6,4},{8,6},{10,8},{12,10},{14,12},{16,14},{18,... | collective-permute-start | bytes 196616 | tf_op jit(solution)/shard_map/ppermute | solution.py:75
  55.6 6.4 %collective-permute-start.12 = (bf16[4,8,1024]{2,1,0:T(8,128)(2,1)S(1)}, bf16[4,8,1024]{2,1,0:T(8,128)(2,1)S(1)}, u32[]{:S(2)}, u32[]{:S(2)}) collective-permute-start(bf16[4,8,1024]{2,1,0:T(8,128)(2,1)S(1)} %collective-permute-done.10), channel_id=1, source_target_pairs={{0,2},{2,4},{4,6},{6,8},{8,10},{10,12},{12,14},{14,16},{16,18},{18... | collective-permute-start | bytes 196616 | tf_op jit(solution)/shard_map/ppermute | solution.py:68
  55.6 6.4 %collective-permute-start.13 = (bf16[4,8,1024]{2,1,0:T(8,128)(2,1)S(1)}, bf16[4,8,1024]{2,1,0:T(8,128)(2,1)S(1)}, u32[]{:S(2)}, u32[]{:S(2)}) collective-permute-start(bf16[4,8,1024]{2,1,0:T(8,128)(2,1)S(1)} %collective-permute-done.11), channel_id=1, source_target_pairs={{0,30},{2,0},{4,2},{6,4},{8,6},{10,8},{12,10},{14,12},{16,14},{18,... | collective-permute-start | bytes 196616 | tf_op jit(solution)/shard_map/ppermute | solution.py:75
  61.9 6.4 %collective-permute-start.14 = (bf16[4,8,1024]{2,1,0:T(8,128)(2,1)S(1)}, bf16[4,8,1024]{2,1,0:T(8,128)(2,1)S(1)}, u32[]{:S(2)}, u32[]{:S(2)}) collective-permute-start(bf16[4,8,1024]{2,1,0:T(8,128)(2,1)S(1)} %collective-permute-done.12), channel_id=1, source_target_pairs={{0,2},{2,4},{4,6},{6,8},{8,10},{10,12},{12,14},{14,16},{16,18},{18... | collective-permute-start | bytes 196616 | tf_op jit(solution)/shard_map/ppermute | solution.py:68
  68.4 20.0 %copy-start.3 = (u32[32]{0:T(128)S(1)}, u32[32]{0:T(128)}, u32[]{:S(2)}) copy-start(u32[32]{0:T(128)} %constant.169) | copy-start | bytes 388
  87.7 0.7 copy-start.1
Sparse Core Ops, SparseCore 0:
  88.5 19.1 all-reduce.2
